TPU v7x, 512 devices: a whole 4x4x16 slice. The times are simulated.
512 devices in a mesh: aux: 128 (over z, x_hi, y), occ: 4 (over x_lo, core).
Axes of the slice: x: 4 (x_hi: 2, x_lo: 2; x = x_hi * 2 + x_lo), y: 4, z: 16, core: 2. Of those that a mesh axis runs over, the one named last changes fastest.
Arguments:
- integrals: bfloat16 [2304, 32, 6144], P('aux', None, 'occ'), may hold values from -6 to 6
- coefficients: bfloat16 [6144, 48], P('occ'), may hold values from -0.29882812 to 0.29882812
- screening: int32 [32, 48], replicated, may hold values 0 or 1
- metric_factor: bfloat16 [2304, 2304], P('aux'), may hold values from -2 to 4
Outputs:
- gamma_block: bfloat16 [2304, 32, 6144], P('aux', 'occ')
All inputs are finite; a program needn't handle non-finite values.
Results may differ from a plain program's by a relative error of at most 0.0057.
Values may be sent and summed in bfloat16 or wider, within the bound.
A program may use at most 64 MiB of HBM per device.

v0:
```python
import jax
import jax.numpy as jnp
from jax import lax
from jax.sharding import PartitionSpec as P

TILE = 128


def on_device(integrals, coefficients, screening, metric_factor):
    aux_dev, rows_all, basis_part = integrals.shape
    occ_count = coefficients.shape[1]
    occ_size = lax.axis_size("occ")
    occ_index = lax.axis_index("occ")
    rows_dev = rows_all // occ_size
    tiles_part = basis_part // TILE
    screen_tiles = screening.astype(jnp.bfloat16)
    part_tiles = lax.dynamic_slice_in_dim(screen_tiles, occ_index * tiles_part, tiles_part, 1)
    part_screen = jnp.repeat(part_tiles, TILE, axis=1)
    masked = integrals * part_screen[None]
    partial_value = jnp.einsum(
        "pmn,ni->pmi", masked, coefficients, preferred_element_type=jnp.float32
    )
    partial_value = partial_value.reshape(aux_dev, rows_all * occ_count)
    half_transformed = lax.psum_scatter(
        partial_value, "occ", scatter_dimension=1, tiled=True
    ).astype(jnp.bfloat16)
    fitted = jnp.dot(
        metric_factor,
        lax.all_gather(half_transformed, "aux", axis=0, tiled=True),
        preferred_element_type=jnp.float32,
    ).astype(jnp.bfloat16)
    whole_coefficients = lax.all_gather(coefficients, "occ", axis=0, tiled=True)
    own_tiles = lax.dynamic_slice_in_dim(screen_tiles, occ_index * rows_dev, rows_dev, 0)
    own_screen = jnp.repeat(own_tiles, TILE, axis=1).astype(jnp.float32)
    flattened = fitted.reshape(aux_dev * rows_dev, occ_count)
    product = lax.dot_general(
        flattened, whole_coefficients, (((1,), (1,)), ((), ())), preferred_element_type=jnp.float32
    )
    product = product.reshape(aux_dev, rows_dev, whole_coefficients.shape[0])
    return (product * own_screen[None]).astype(jnp.bfloat16)


def solution(mesh):
    return jax.shard_map(
        on_device,
        mesh=mesh,
        in_specs=(P("aux", None, "occ"), P("occ", None), P(), P("aux", None)),
        out_specs=P("aux", "occ", None),
        check_vma=False,
    )
```

profile of v0, /device:TPU:8, one launch (start us, length us, event | category | flops | bytes accessed | tf_op | source)
XLA Modules:
  0.0 273.1 jit_solution(12376429188576232641)
XLA Ops:
  6.5 0.0 copy-start
  6.5 0.0 reduce-scatter.2.cloned.1.call-start
  6.5 0.8 convert_element_type.26
  7.3 0.1 constant_dynamic-slice_fusion
  7.4 0.1 broadcast_in_dim.7
  7.5 0.0 copy-start.1
  7.6 2.1 fusion.1
  9.7 0.8 reshape.15
  10.5 0.0 reduce-scatter.2.cloned.1.call-update
  10.6 0.0 all-gather.3.cloned.1.call-start
  10.6 29.2 %reduce-scatter.2.cloned.1.call-done = f32[18,384]{1,0:T(8,128)} async-done(((f32[18,1536]{1,0:T(8,128)}), f32[18,384]{1,0:T(8,128)}) %reduce-scatter.2.cloned.1.call-update) | async-done | bytes 27664 | tf_op jit(solution)/shard_map/reduce_scatter | solution.py:24
  39.8 1.4 convert_bitcast_fusion
  41.1 0.0 all-gather.3.cloned.1.call-update
  41.2 0.1 copy.7
  41.3 0.0 copy-done.1
  41.3 7.7 %all_gather.7 = bf16[6144,48]{0,1:T(8,128)(2,1)S(1)} all-gather(bf16[1536,48]{0,1:T(8,128)(2,1)S(1)} %copy-done.1), channel_id=1, replica_groups=mesh['aux'=128,'occ'=4] {'occ'}, dimensions={0}, use_global_device_ids=true | all-gather | bytes 737280 | tf_op jit(solution)/shard_map/all_gather | solution.py:32
  48.9 0.1 broadcast_bitcast_fusion
  49.0 212.3 %all-gather.3.cloned.1.call-done = bf16[128,18,384]{2,1,0:T(8,128)(2,1)} async-done(((bf16[1,18,384]{2,1,0:T(8,128)(2,1)}), bf16[128,18,384]{2,1,0:T(8,128)(2,1)}) %all-gather.3.cloned.1.call-update) | async-done | bytes 1769488 | tf_op jit(solution)/shard_map/all_gather | solution.py:29
  261.3 2.6 reshape.17
  264.0 0.0 copy-done
  264.0 0.3 fusion.3
  264.3 0.1 dot_general.13
  264.5 1.8 fusion
  (2 shorter events, 0.0 us)
Async XLA Ops:
  6.5 257.4 %copy-start = (bf16[18,2304]{1,0:T(8,128)(2,1)S(1)}, bf16[18,2304]{1,0:T(8,128)(2,1)}, u32[]{:S(2)}) copy-start(bf16[18,2304]{1,0:T(8,128)(2,1)} %param.7) | copy-start | bytes 248836
  6.5 33.2 %reduce-scatter.2.cloned.1.call-start = ((), (), s32[]{:S(2)}) async-start(), calls=%async_computation.1 | async-start | bytes 184320 | tf_op jit(solution)/shard_map/reduce_scatter | solution.py:24
  7.5 33.7 %copy-start.1 = (bf16[1536,48]{0,1:T(8,128)(2,1)S(1)}, bf16[1536,48]{0,1:T(8,128)(2,1)}, u32[]{:S(2)}) copy-start(bf16[1536,48]{0,1:T(8,128)(2,1)} %param.5) | copy-start | bytes 442372
  10.6 250.8 %all-gather.3.cloned.1.call-start = ((), (), s32[]{:S(2)}) async-start(), calls=%async_computation.2 | async-start | bytes 2377728 | tf_op jit(solution)/shard_map/all_gather | solution.py:29
Sparse Core Ops, SparseCore 0:
  10.7 29.0 reduce-scatter.1
  44.2 217.0 all-gather.2
where the time goes:
time: 273 us
  waiting for transfers between devices  241 us (88%)
  between operations  13.5 us (5%)
  blocking collectives  7.67 us (3%)
  matrix products  4.27 us (2%)
  local copies, waits for them, and re-layouts  4.02 us (1%)
    all_gather x1, waiting for transfers between devices, on_device(): lax.all_gather(half_transformed, 'aux', axis=0, tiled=True)  212 us
    reduce_scatter x1, waiting for transfers between devices, on_device(): lax.psum_scatter(partial_value, 'occ', scatter_dimension=1, tiled=True)  29.2 us
    all_gather x1, blocking collectives, on_device(): whole_coefficients = lax.all_gather(coefficients, 'occ', axis=0, tiled=True)  7.67 us
  transfers between devices with their start and end apart: 2, of which 2 were waited for; matrix products, arithmetic and copies ran while one was open for 0% of the time, Pallas kernels for 0%

commit v1 on v0

--- a/solution.py
+++ b/solution.py
@@ -26,7 +26,10 @@
     ).astype(jnp.bfloat16)
     fitted = jnp.dot(
         metric_factor,
-        lax.all_gather(half_transformed, "aux", axis=0, tiled=True),
+        jnp.concatenate(
+            lax.all_to_all(jnp.stack([half_transformed] * lax.axis_size("aux")), "aux", 0, 0),
+            axis=0,
+        ),
         preferred_element_type=jnp.float32,
     ).astype(jnp.bfloat16)
     whole_coefficients = lax.all_gather(coefficients, "occ", axis=0, tiled=True)

time: 273 us -> 185 us (0.68)
  the two profiles are of different devices: /device:TPU:8 before, /device:TPU:40 now
where the time goes in v1:
time: 185 us; the launch traced here: 184 us
  waiting for transfers between devices  132 us (71%)
  starting transfers between devices  19.1 us (10%)
  between operations  13.5 us (7%)
  blocking collectives  8.08 us (4%)
  local copies, waits for them, and re-layouts  5.63 us (3%)
  matrix products  4.24 us (2%)
    all_to_all x1, waiting for transfers between devices, on_device(): lax.all_to_all(jnp.stack([half_transformed] * lax.axis_size('aux')), 'aux...  104 us
    reduce_scatter x1, waiting for transfers between devices, on_device(): lax.psum_scatter(partial_value, 'occ', scatter_dimension=1, tiled=True)  28.9 us
    all_to_all x1, starting transfers between devices, on_device(): lax.all_to_all(jnp.stack([half_transformed] * lax.axis_size('aux')), 'aux...  19.1 us
    all_gather x1, blocking collectives, on_device(): whole_coefficients = lax.all_gather(coefficients, 'occ', axis=0, tiled=True)  8.08 us
  transfers between devices with their start and end apart: 2, of which 2 were waited for; matrix products, arithmetic and copies ran while one was open for 0% of the time, Pallas kernels for 0%

profile of v1, /device:TPU:40, one launch (start us, length us, event | category | flops | bytes accessed | tf_op | source)
XLA Modules:
  0.0 184.4 jit_solution(12946130230778986033)
XLA Ops:
  6.5 0.0 copy-start
  6.5 0.0 reduce-scatter.2.cloned.1.call-start
  6.5 0.8 convert_element_type.26
  7.3 0.1 constant_dynamic-slice_fusion
  7.4 0.1 broadcast_in_dim.7
  7.5 2.1 %fusion.1 = f32[18,32,48]{2,1,0:T(8,128)S(1)} fusion(bf16[18,32,1536]{2,1,0:T(8,128)(2,1)} %param.4, bf16[32,1536]{1,0:T(8,128)(2,1)S(1)} %bitcast.18, bf16[1536,48]{0,1:T(8,128)(2,1)} %param.5), kind=kOutput, calls=%fused_computation.2 | convolution fusion | flops 85819392 | bytes 2125824 | tf_op jit(solution)/shard_map/pmn,ni->pmi/dot_general | solution.py:20
  9.6 0.8 reshape.20
  10.5 0.0 reduce-scatter.2.cloned.1.call-update
  10.5 28.9 %reduce-scatter.2.cloned.1.call-done = f32[18,384]{1,0:T(8,128)} async-done(((f32[18,1536]{1,0:T(8,128)}), f32[18,384]{1,0:T(8,128)}) %reduce-scatter.2.cloned.1.call-update) | async-done | bytes 27664 | tf_op jit(solution)/shard_map/reduce_scatter | solution.py:24
  39.4 0.8 convert_element_type.27
  40.1 1.6 stack.2
  41.8 0.0 copy-start.1
  41.8 19.1 %all-to-all-start = ((bf16[128,18,384]{2,1,0:T(8,128)(2,1)}), bf16[128,18,384]{2,1,0:T(8,128)(2,1)}, u32[]{:S(2)}, u32[]{:S(2)}) async-start(bf16[128,18,384]{2,1,0:T(8,128)(2,1)} %stack.2), calls=%async_computation.1 | async-start | bytes 4718592 | tf_op jit(solution)/shard_map/all_to_all | solution.py:30
  60.9 0.1 copy.6
  60.9 0.0 copy-done.1
  60.9 8.1 %all_gather.3 = bf16[6144,48]{0,1:T(8,128)(2,1)S(1)} all-gather(bf16[1536,48]{0,1:T(8,128)(2,1)S(1)} %copy-done.1), channel_id=1, replica_groups=mesh['aux'=128,'occ'=4] {'occ'}, dimensions={0}, use_global_device_ids=true | all-gather | bytes 737280 | tf_op jit(solution)/shard_map/all_gather | solution.py:35
  69.0 0.1 broadcast_bitcast_fusion
  69.1 103.5 %all-to-all-done = bf16[128,18,384]{2,1,0:T(8,128)(2,1)} async-done(((bf16[128,18,384]{2,1,0:T(8,128)(2,1)}), bf16[128,18,384]{2,1,0:T(8,128)(2,1)}, u32[]{:S(2)}, u32[]{:S(2)}) %all-to-all-start) | async-done | bytes 1769504 | tf_op jit(solution)/shard_map/all_to_all | solution.py:30
  172.6 2.6 %reshape.21 = bf16[2304,384]{1,0:T(8,128)(2,1)S(1)} reshape(bf16[128,18,384]{2,1,0:T(8,128)(2,1)} %all-to-all-done) | data formatting | bytes 3538944 | tf_op jit(solution)/shard_map/reshape | solution.py:29
  175.3 0.0 copy-done
  175.3 0.3 fusion.3
  175.7 0.1 dot_general.13
  175.8 1.8 fusion
  (2 shorter events, 0.0 us)
Async XLA Ops:
  6.5 168.8 %copy-start = (bf16[18,2304]{1,0:T(8,128)(2,1)S(1)}, bf16[18,2304]{1,0:T(8,128)(2,1)}, u32[]{:S(2)}) copy-start(bf16[18,2304]{1,0:T(8,128)(2,1)} %param.7) | copy-start | bytes 248836
  6.5 32.8 %reduce-scatter.2.cloned.1.call-start = ((), (), s32[]{:S(2)}) async-start(), calls=%async_computation.2 | async-start | bytes 184320 | tf_op jit(solution)/shard_map/reduce_scatter | solution.py:24
  41.8 19.2 %copy-start.1 = (bf16[1536,48]{0,1:T(8,128)(2,1)S(1)}, bf16[1536,48]{0,1:T(8,128)(2,1)}, u32[]{:S(2)}) copy-start(bf16[1536,48]{0,1:T(8,128)(2,1)} %param.5) | copy-start | bytes 442372
  41.8 130.9 %all-to-all-start = ((bf16[128,18,384]{2,1,0:T(8,128)(2,1)}), bf16[128,18,384]{2,1,0:T(8,128)(2,1)}, u32[]{:S(2)}, u32[]{:S(2)}) async-start(bf16[128,18,384]{2,1,0:T(8,128)(2,1)} %stack.2), calls=%async_computation.1 | async-start | bytes 4718592 | tf_op jit(solution)/shard_map/all_to_all | solution.py:30
Sparse Core Ops, SparseCore 0:
  10.6 28.7 reduce-scatter.1
